TPU v7x, 32 devices: a whole 2x2x4 slice. The times are simulated.
32 devices in a mesh: dp: 8 (over y, x, core), tensor: 4 (over z).
Axes of the slice: x: 2, y: 2, z: 4, core: 2. Of those that a mesh axis runs over, the one named last changes fastest.
Arguments:
- tokens: bfloat16 [20480, 768], P(('dp', 'tensor')), may hold values from -6 to 6
- visible_counts: int32 [256], P('dp'), may hold values from 20 to 78, as said below
- norm_one_gain: float32 [768], replicated, may hold values from 0.1 to 1.9
- norm_one_shift: float32 [768], replicated, may hold values from -1.8 to 1.8
- input_weight: bfloat16 [768, 3, 768], P(None, None, 'tensor'), may hold values from -0.21875 to 0.21875
- input_bias: bfloat16 [2, 768], P(None, 'tensor'), may hold values from -1.796875 to 1.796875
- mixer_weight: bfloat16 [768, 768], P('tensor'), may hold values from -1.25 to 1.25
- mixer_bias: float32 [768], replicated, may hold values from -1.8 to 1.8
- norm_two_gain: float32 [768], replicated, may hold values from 0.1 to 1.9
- norm_two_shift: float32 [768], replicated, may hold values from -1.8 to 1.8
- up_weight: bfloat16 [768, 3072], P(None, 'tensor'), may hold values from -0.21875 to 0.21875
- up_bias: bfloat16 [3072], P('tensor'), may hold values from -1.796875 to 1.796875
- down_weight: bfloat16 [3072, 768], P('tensor'), may hold values from -0.109375 to 0.109375
- down_bias: float32 [768], replicated, may hold values from -1.8 to 1.8
- output_grad: bfloat16 [20480, 768], P(('dp', 'tensor')), may hold values from -6 to 6
Outputs:
- block_output: bfloat16 [20480, 768], P(('dp', 'tensor'))
- grad_tokens: float32 [20480, 768], P(('dp', 'tensor'))
- grad_norm_one_gain: float32 [768], replicated
- grad_norm_one_shift: float32 [768], replicated
- grad_input_weight: float32 [768, 3, 768], P(None, None, 'tensor')
- grad_input_bias: float32 [2, 768], P(None, 'tensor')
- grad_mixer_weight: float32 [768, 768], P('tensor')
- grad_mixer_bias: float32 [768], replicated
- grad_norm_two_gain: float32 [768], replicated
- grad_norm_two_shift: float32 [768], replicated
- grad_up_weight: float32 [768, 3072], P(None, 'tensor')
- grad_up_bias: float32 [3072], P('tensor')
- grad_down_weight: float32 [3072, 768], P('tensor')
- grad_down_bias: float32 [768], replicated
Inputs may be any that keep to these rules, and one draw needn't show every extreme that they name: `visible_counts`: each image has 20 to 78 visible patches; some image has exactly 78 and some exactly 20.
All inputs are finite; a program needn't handle non-finite values.
Results may differ from a plain program's by a relative error of at most 0.014.
Values may be sent and summed in bfloat16 or wider, within the bound.
No kernel may reach another device: no remote copies, remote signals or barrier semaphores. Data moves between devices by JAX's collectives and lax.ppermute only.
A program may use at most 128 MiB of HBM per device.

v0:
```python
import jax
import jax.numpy as jnp
from jax import lax
from jax.sharding import PartitionSpec as P

HD = 64
SLOTS = 80
masked_score = -1000000000.0


def layer_norm(inputs, norm_gain, norm_shift):
    center = inputs - jnp.mean(inputs, axis=-1, keepdims=True)
    spread = jnp.mean(center * center, axis=-1, keepdims=True)
    return center * lax.rsqrt(spread + 1e-06) * norm_gain + norm_shift


def norm_back(inputs, norm_gain, norm_shift, grad_normed):
    unused, pullback = jax.vjp(layer_norm, inputs, norm_gain, norm_shift)
    return pullback(grad_normed)


def gelu_exact(inputs):
    return jax.nn.gelu(inputs, approximate=False)


def split_heads(flat, slot_count, head_dim):
    return flat.reshape(
        flat.shape[0] // slot_count, slot_count, flat.shape[1] // head_dim, head_dim
    )


def visible_keys(counts, slot_count):
    return (lax.broadcasted_iota(jnp.int32, (counts.shape[0], slot_count), 1) < counts[:, None])[
        :, None, None, :
    ]


def project_inputs(normed_rows, weight_in, bias_in, slot_count, head_dim):
    columns = weight_in.shape[2]
    product = jnp.dot(
        normed_rows,
        weight_in.reshape(weight_in.shape[0], 3 * columns),
        preferred_element_type=jnp.float32,
    ).reshape(-1, 3, columns)
    queries = (product[:, 0] + bias_in[0]).astype(jnp.bfloat16)
    key_rows = product[:, 1].astype(jnp.bfloat16)
    values = (product[:, 2] + bias_in[1]).astype(jnp.bfloat16)
    return (
        split_heads(queries, slot_count, head_dim),
        split_heads(key_rows, slot_count, head_dim),
        split_heads(values, slot_count, head_dim),
    )


def attend(queries, key_rows, values, counts):
    factor = queries.shape[-1] ** (-0.5)
    scores = (
        jnp.einsum("bqhd,bkhd->bhqk", queries, key_rows, preferred_element_type=jnp.float32)
        * factor
    )
    scores = jnp.where(visible_keys(counts, key_rows.shape[1]), scores, masked_score)
    maxima = jnp.max(scores, axis=-1, keepdims=True)
    exponent = jnp.exp(scores - maxima)
    totals = jnp.sum(exponent, axis=-1, keepdims=True)
    soft_low = (exponent / totals).astype(jnp.bfloat16)
    blended = jnp.einsum("bhqk,bkhd->bqhd", soft_low, values, preferred_element_type=jnp.float32)
    return (blended, maxima + jnp.log(totals))


def attend_back(queries, key_rows, values, counts, log_totals, grad_blend):
    factor = queries.shape[-1] ** (-0.5)
    scores = (
        jnp.einsum("bqhd,bkhd->bhqk", queries, key_rows, preferred_element_type=jnp.float32)
        * factor
    )
    scores = jnp.where(visible_keys(counts, key_rows.shape[1]), scores, masked_score)
    soft = jnp.exp(scores - log_totals)
    soft_low = soft.astype(jnp.bfloat16)
    grad_values = jnp.einsum(
        "bhqk,bqhd->bkhd", soft_low, grad_blend, preferred_element_type=jnp.float32
    )
    grad_soft = jnp.einsum(
        "bqhd,bkhd->bhqk", grad_blend, values, preferred_element_type=jnp.float32
    )
    grad_scores = soft * (grad_soft - jnp.sum(grad_soft * soft, axis=-1, keepdims=True))
    grad_low = grad_scores.astype(jnp.bfloat16)
    grad_queries = (
        jnp.einsum("bhqk,bkhd->bqhd", grad_low, key_rows, preferred_element_type=jnp.float32)
        * factor
    )
    grad_keys = (
        jnp.einsum("bhqk,bqhd->bkhd", grad_low, queries, preferred_element_type=jnp.float32)
        * factor
    )
    return (grad_queries, grad_keys, grad_values)


def mlp_back(normed_rows, hidden_pre, active, grad_rows, weight_down):
    grad_down = jnp.einsum("rf,rd->fd", active, grad_rows, preferred_element_type=jnp.float32)
    grad_active = jnp.einsum(
        "rd,fd->rf", grad_rows, weight_down, preferred_element_type=jnp.float32
    )
    unused, pullback = jax.vjp(gelu_exact, hidden_pre)
    grad_pre = pullback(grad_active)[0]
    grad_up_b = jnp.sum(grad_pre, axis=0)
    grad_pre_low = grad_pre.astype(jnp.bfloat16)
    grad_up = jnp.einsum("rd,rf->df", normed_rows, grad_pre_low, preferred_element_type=jnp.float32)
    return (grad_down, grad_up, grad_up_b, grad_pre_low)


def mixer_back(
    normed_rows,
    queries,
    key_rows,
    values,
    counts,
    log_totals,
    grad_rows,
    blend_low,
    weight_mix,
    slot_count,
    head_dim,
):
    row_total = blend_low.shape[0]
    grad_mix = jnp.einsum("rc,rd->cd", blend_low, grad_rows, preferred_element_type=jnp.float32)
    grad_blend = jnp.einsum(
        "rd,cd->rc", grad_rows, weight_mix, preferred_element_type=jnp.float32
    ).astype(jnp.bfloat16)
    grad_queries, grad_keys, grad_values = attend_back(
        queries, key_rows, values, counts, log_totals, split_heads(grad_blend, slot_count, head_dim)
    )
    grad_queries = grad_queries.reshape(row_total, -1)
    grad_keys = grad_keys.reshape(row_total, -1)
    grad_values = grad_values.reshape(row_total, -1)
    grad_bias_in = jnp.stack([jnp.sum(grad_queries, axis=0), jnp.sum(grad_values, axis=0)])
    grad_projected = jnp.stack([grad_queries, grad_keys, grad_values], axis=1).astype(jnp.bfloat16)
    grad_weight_in = jnp.einsum(
        "rd,rjc->djc", normed_rows, grad_projected, preferred_element_type=jnp.float32
    )
    return (grad_mix, grad_bias_in, grad_weight_in, grad_projected)


def local(
    tokens,
    visible_counts,
    norm_one_gain,
    norm_one_shift,
    input_weight,
    input_bias,
    mixer_weight,
    mixer_bias,
    norm_two_gain,
    norm_two_shift,
    up_weight,
    up_bias,
    down_weight,
    down_bias,
    output_grad,
):
    slot_count = SLOTS
    head_dim = HD
    inputs = tokens.astype(jnp.float32)
    grad_output = output_grad.astype(jnp.float32)
    low_one = layer_norm(inputs, norm_one_gain, norm_one_shift).astype(jnp.bfloat16)
    whole_one = lax.all_gather(low_one, "tensor", axis=0, tiled=True)
    queries, key_rows, values = project_inputs(
        whole_one, input_weight, input_bias, slot_count, head_dim
    )
    blended, log_totals = attend(queries, key_rows, values, visible_counts)
    blend_low = blended.reshape(whole_one.shape[0], -1).astype(jnp.bfloat16)
    first_sum = (
        inputs
        + lax.psum_scatter(
            jnp.dot(blend_low, mixer_weight, preferred_element_type=jnp.float32),
            "tensor",
            scatter_dimension=0,
            tiled=True,
        )
        + mixer_bias
    )
    low_two = layer_norm(first_sum, norm_two_gain, norm_two_shift).astype(jnp.bfloat16)
    whole_two = lax.all_gather(low_two, "tensor", axis=0, tiled=True)
    hidden_pre = jnp.dot(whole_two, up_weight, preferred_element_type=jnp.float32) + up_bias
    active = gelu_exact(hidden_pre).astype(jnp.bfloat16)
    result = (
        first_sum
        + lax.psum_scatter(
            jnp.dot(active, down_weight, preferred_element_type=jnp.float32).astype(jnp.bfloat16),
            "tensor",
            scatter_dimension=0,
            tiled=True,
        ).astype(jnp.float32)
        + down_bias
    )
    whole_grad = lax.all_gather(output_grad, "tensor", axis=0, tiled=True)
    grad_down, grad_up, grad_up_b, grad_pre_low = mlp_back(
        whole_two, hidden_pre, active, whole_grad, down_weight
    )
    grad_normed_two = lax.psum_scatter(
        jnp.einsum("rf,df->rd", grad_pre_low, up_weight, preferred_element_type=jnp.float32),
        "tensor",
        scatter_dimension=0,
        tiled=True,
    )
    grad_first, grad_gain_two, grad_shift_two = norm_back(
        first_sum, norm_two_gain, norm_two_shift, grad_normed_two
    )
    grad_first = grad_output + grad_first
    whole_first = lax.all_gather(grad_first.astype(jnp.bfloat16), "tensor", axis=0, tiled=True)
    grad_mix, grad_bias_in, grad_weight_in, grad_projected = mixer_back(
        whole_one,
        queries,
        key_rows,
        values,
        visible_counts,
        log_totals,
        whole_first,
        blend_low,
        mixer_weight,
        slot_count,
        head_dim,
    )
    grad_normed_one = lax.psum_scatter(
        jnp.einsum(
            "rjc,djc->rd", grad_projected, input_weight, preferred_element_type=jnp.float32
        ).astype(jnp.bfloat16),
        "tensor",
        scatter_dimension=0,
        tiled=True,
    ).astype(jnp.float32)
    weight_terms = (grad_weight_in, grad_bias_in, grad_mix, grad_up, grad_up_b, grad_down)
    grad_inputs, grad_gain_one, grad_shift_one = norm_back(
        inputs, norm_one_gain, norm_one_shift, grad_normed_one
    )
    grad_tokens = grad_first + grad_inputs
    sum_gain_one, sum_shift_one, sum_mix_bias, sum_gain_two, sum_shift_two, sum_down_bias = (
        lax.psum(
            (
                grad_gain_one,
                grad_shift_one,
                jnp.sum(grad_first, axis=0),
                grad_gain_two,
                grad_shift_two,
                jnp.sum(grad_output, axis=0),
            ),
            ("dp", "tensor"),
        )
    )
    sum_weight_in, sum_bias_in, sum_mix, sum_up, sum_up_b, sum_down = lax.psum(
        (
            weight_terms[0],
            weight_terms[1],
            weight_terms[2],
            weight_terms[3],
            weight_terms[4],
            weight_terms[5],
        ),
        "dp",
    )
    return (
        result.astype(jnp.bfloat16),
        grad_tokens,
        sum_gain_one,
        sum_shift_one,
        sum_weight_in,
        sum_bias_in,
        sum_mix,
        sum_mix_bias,
        sum_gain_two,
        sum_shift_two,
        sum_up,
        sum_up_b,
        sum_down,
        sum_down_bias,
    )


def solution(mesh):
    in_specs = (
        P(("dp", "tensor"), None),
        P("dp"),
        P(),
        P(),
        P(None, None, "tensor"),
        P(None, "tensor"),
        P("tensor", None),
        P(),
        P(),
        P(),
        P(None, "tensor"),
        P("tensor"),
        P("tensor", None),
        P(),
        P(("dp", "tensor"), None),
    )
    out_specs = (
        P(("dp", "tensor"), None),
        P(("dp", "tensor"), None),
        P(),
        P(),
        P(None, None, "tensor"),
        P(None, "tensor"),
        P("tensor", None),
        P(),
        P(),
        P(),
        P(None, "tensor"),
        P("tensor"),
        P("tensor", None),
        P(),
    )
    return jax.shard_map(local, mesh=mesh, in_specs=in_specs, out_specs=out_specs, check_vma=False)
```

profile of v0, /device:TPU:0, one launch (start us, length us, event | category | flops | bytes accessed | tf_op | source)
XLA Modules:
  0.0 1010.1 jit_solution(16693348201039939642)
XLA Ops:
  14.6 79.0 %all-gather.5.cloned.1.call-done = bf16[2560,768]{1,0:T(8,128)(2,1)} async-done(((bf16[640,768]{1,0:T(8,128)(2,1)}), bf16[2560,768]{1,0:T(8,128)(2,1)}) %all-gather.5.cloned.1.call-update) | async-done | bytes 3932176 | tf_op jit(solution)/shard_map/all_gather | solution.py:165
  93.6 4.6 fusion.6
  104.7 4.7 squeeze.4
  113.5 5.2 fusion.57
  135.3 134.9 %reduce-scatter.5.cloned.1.call-done = f32[640,768]{1,0:T(8,128)} async-done(((f32[2560,768]{1,0:T(8,128)}), f32[640,768]{1,0:T(8,128)}) %reduce-scatter.5.cloned.1.call-update) | async-done | bytes 1966096 | tf_op jit(solution)/shard_map/reduce_scatter | solution.py:173
  274.7 76.5 %all-gather.7.cloned.1.call-done = bf16[2560,768]{1,0:T(8,128)(2,1)} async-done(((bf16[640,768]{1,0:T(8,128)(2,1)}), bf16[2560,768]{1,0:T(8,128)(2,1)}) %all-gather.7.cloned.1.call-update) | async-done | bytes 3932176 | tf_op jit(solution)/shard_map/all_gather | solution.py:182
  351.2 9.0 fusion.59
  360.2 67.5 %all-gather.9.cloned.1.call-done = bf16[2560,768]{1,0:T(8,128)(2,1)} async-done(((bf16[640,768]{1,0:T(8,128)(2,1)}), bf16[2560,768]{1,0:T(8,128)(2,1)}) %all-gather.9.cloned.1.call-update) | async-done | bytes 3932176 | tf_op jit(solution)/shard_map/all_gather | solution.py:195
  427.6 23.8 %fusion.51 = (f32[768]{0:T(1024)S(1)}, bf16[2560,768]{1,0:T(8,128)(2,1)S(1)}, f32[2560,768]{1,0:T(8,128)}) fusion(f32[2560,768]{1,0:T(8,128)} %fusion.59, f32[768]{0:T(1024)S(1)} %convert_element_type.88, bf16[2560,768]{1,0:T(8,128)(2,1)} %all-gather.9.cloned.1.call-done, bf16[768,768]{1,0:T(8,128)(2,1)S(1)} %copy-done), kind=kOutput, calls=%fused_computation.106 | convolution fusion | flops 3165388032 | bytes 24778752 | tf_op jit(solution)/shard_map/rd,fd->rf/dot_general | solution.py:100
  453.3 5.4 fusion.29
  459.2 8.0 multiply_convert_fusion
  469.2 4.7 convolution_convert_fusion
  473.9 119.7 %reduce-scatter.9.cloned.1.call-done = f32[640,768]{1,0:T(8,128)} async-done(((f32[2560,768]{1,0:T(8,128)}), f32[640,768]{1,0:T(8,128)}) %reduce-scatter.9.cloned.1.call-update) | async-done | bytes 1966096 | tf_op jit(solution)/shard_map/reduce_scatter | solution.py:199
  596.0 73.1 %reduce-scatter.7.cloned.1.call-done = bf16[640,768]{1,0:T(8,128)(2,1)} async-done(((bf16[2560,768]{1,0:T(8,128)(2,1)}), bf16[640,768]{1,0:T(8,128)(2,1)}) %reduce-scatter.7.cloned.1.call-update) | async-done | bytes 983056 | tf_op jit(solution)/shard_map/reduce_scatter | solution.py:187
  675.4 76.9 %all-gather.11.cloned.1.call-done = bf16[2560,768]{1,0:T(8,128)(2,1)} async-done(((bf16[640,768]{1,0:T(8,128)(2,1)}), bf16[2560,768]{1,0:T(8,128)(2,1)}) %all-gather.11.cloned.1.call-update) | async-done | bytes 3932176 | tf_op jit(solution)/shard_map/all_gather | solution.py:209
  752.2 4.5 convolution_convert_fusion.1
  760.0 7.1 multiply_reduce_fusion
  800.9 4.7 bitcast_convert_fusion
  806.0 8.1 fusion.27
  814.2 4.8 fusion.61
  829.5 14.4 %all-reduce.1 = (f32[2,192]{1,0:T(2,128)}, f32[768]{0:T(1024)}) all-reduce(f32[2,192]{1,0:T(2,128)S(1)} %pad_maximum_fusion, f32[768]{0:T(1024)S(1)} %get-tuple-element.37), channel_id=1, replica_groups=mesh['dp'=8,'tensor'=4] {'dp'}, use_global_device_ids=true, to_apply=%region_22.23 | all-reduce | flops 1152 | bytes 9216 | tf_op jit(solution)/shard_map/psum | solution.py:249
  843.9 33.2 %reduce-scatter.11.cloned.1.call-done = bf16[640,768]{1,0:T(8,128)(2,1)} async-done(((bf16[2560,768]{1,0:T(8,128)(2,1)}), bf16[640,768]{1,0:T(8,128)(2,1)}) %reduce-scatter.11.cloned.1.call-update) | async-done | bytes 983056 | tf_op jit(solution)/shard_map/reduce_scatter | solution.py:223
  883.8 41.7 %all-reduce = (f32[768]{0:T(1024)}, f32[768]{0:T(1024)}, f32[768]{0:T(1024)}, f32[768]{0:T(1024)}, f32[768]{0:T(1024)}, /*index=5*/f32[768]{0:T(1024)}) all-reduce(f32[768]{0:T(1024)S(1)} %get-tuple-element.16, f32[768]{0:T(1024)S(1)} %get-tuple-element.21, ...), channel_id=1, replica_groups=mesh['dp'=8,'tensor'=4] {'dp','tensor'}, use_global_device_ids=true, to_apply=%region_16.17 | all-reduce | flops 4608 | bytes 36864 | tf_op jit(solution)/shard_map/psum | solution.py:237
  925.4 71.1 %all-reduce.5.cloned.1.call-done = (f32[768,3,192]{0,2,1:T(8,128)}, f32[192,768]{1,0:T(8,128)}, f32[768,768]{1,0:T(8,128)}, f32[768,768]{1,0:T(8,128)}) async-done(((f32[768,3,192]{0,2,1:T(8,128)}, f32[192,768]{1,0:T(8,128)}, f32[768,768]{1,0:T(8,128)}, f32[768,768]{1,0:T(8,128)}), (f32[768,3,192]{0,2,1:T(8,128)}, f32[192,768]{1,0:T(8,128)}, f32[768,768]{1,0:T(8,128)}, ...) | async-done | bytes 7077904 | tf_op jit(solution)/shard_map/psum | solution.py:249
  (172 shorter events, 112.8 us)
Async XLA Ops:
  7.2 420.5 %copy-start = (bf16[768,768]{1,0:T(8,128)(2,1)S(1)}, bf16[768,768]{1,0:T(8,128)(2,1)}, u32[]{:S(2)}) copy-start(bf16[768,768]{1,0:T(8,128)(2,1)} %param.27) | copy-start | bytes 3538948
  7.2 86.3 %copy-start.44 = (bf16[768,3,192]{0,2,1:T(8,128)(2,1)S(1)}, bf16[768,3,192]{0,2,1:T(8,128)(2,1)}, u32[]{:S(2)}) copy-start(bf16[768,3,192]{0,2,1:T(8,128)(2,1)} %param.19) | copy-start | bytes 2654212
  7.2 86.3 %all-gather.5.cloned.1.call-start = ((), (), s32[]{:S(2)}) async-start(), calls=%async_computation.4 | async-start | bytes 4915200 | tf_op jit(solution)/shard_map/all_gather | solution.py:165
  14.3 255.9 %reduce-scatter.5.cloned.1.call-start = ((), (), s32[]{:S(2)}) async-start(), calls=%async_computation.5 | async-start | bytes 9830400 | tf_op jit(solution)/shard_map/reduce_scatter | solution.py:173
  104.7 8.9 copy-start.7
  135.2 135.0 %copy-start.35 = (f32[768]{0:T(1024)S(1)}, f32[768]{0:T(1024)}, u32[]{:S(2)}) copy-start(f32[768]{0:T(1024)} %param.22) | copy-start | bytes 9220
  135.2 137.5 %copy-start.34 = (f32[768]{0:T(1024)S(1)}, f32[768]{0:T(1024)}, u32[]{:S(2)}) copy-start(f32[768]{0:T(1024)} %param.23) | copy-start | bytes 9220
  135.2 137.5 %copy-start.36 = (f32[768]{0:T(1024)S(1)}, f32[768]{0:T(1024)}, u32[]{:S(2)}) copy-start(f32[768]{0:T(1024)} %param.24) | copy-start | bytes 9220
  135.3 215.9 %all-gather.7.cloned.1.call-start = ((), (), s32[]{:S(2)}) async-start(), calls=%async_computation.6 | async-start | bytes 4915200 | tf_op jit(solution)/shard_map/all_gather | solution.py:182
  274.1 153.6 %all-gather.9.cloned.1.call-start = ((), (), s32[]{:S(2)}) async-start(), calls=%async_computation.8 | async-start | bytes 4915200 | tf_op jit(solution)/shard_map/all_gather | solution.py:195
  274.6 319.0 %reduce-scatter.9.cloned.1.call-start = ((), (), s32[]{:S(2)}) async-start(), calls=%async_computation.9 | async-start | bytes 9830400 | tf_op jit(solution)/shard_map/reduce_scatter | solution.py:199
  427.6 25.7 %copy-start.43 = (bf16[768,768]{1,0:T(8,128)(2,1)S(1)}, bf16[768,768]{1,0:T(8,128)(2,1)}, u32[]{:S(2)}) copy-start(bf16[768,768]{1,0:T(8,128)(2,1)} %param.25) | copy-start | bytes 3538948
  458.7 210.3 %reduce-scatter.7.cloned.1.call-start = ((), (), s32[]{:S(2)}) async-start(), calls=%async_computation.7 | async-start | bytes 4915200 | tf_op jit(solution)/shard_map/reduce_scatter | solution.py:187
  473.8 195.2 %copy-start.37 = (f32[768]{0:T(1024)S(1)}, f32[768]{0:T(1024)}, u32[]{:S(2)}) copy-start(f32[768]{0:T(1024)} %param.28) | copy-start | bytes 9220
  473.9 278.3 %all-gather.11.cloned.1.call-start = ((), (), s32[]{:S(2)}) async-start(), calls=%async_computation.10 | async-start | bytes 4915200 | tf_op jit(solution)/shard_map/all_gather | solution.py:209
  675.3 201.8 %reduce-scatter.11.cloned.1.call-start = ((), (), s32[]{:S(2)}) async-start(), calls=%async_computation.11 | async-start | bytes 4915200 | tf_op jit(solution)/shard_map/reduce_scatter | solution.py:223
  805.7 190.8 %all-reduce.5.cloned.1.call-start = ((), (), s32[]{:S(2)}) async-start(), calls=%async_computation.12 | async-start | bytes 14155776 | tf_op jit(solution)/shard_map/psum | solution.py:249
  806.0 8.2 copy-start.16
  824.6 52.5 %copy-start.3 = (bf16[640,768]{1,0:T(8,128)(2,1)S(1)}, bf16[640,768]{1,0:T(8,128)(2,1)}, u32[]{:S(2)}) copy-start(bf16[640,768]{1,0:T(8,128)(2,1)} %param.15) | copy-start | bytes 2949124
  824.6 52.5 %copy-start.28 = (f32[640]{0:T(1024)S(1)}, f32[640]{0:T(1024)}, u32[]{:S(2)}) copy-start(f32[640]{0:T(1024)} %copy-done.27) | copy-start | bytes 7684
  824.6 52.5 %copy-start.29 = (f32[768]{0:T(1024)S(1)}, f32[768]{0:T(1024)}, u32[]{:S(2)}) copy-start(f32[768]{0:T(1024)} %param.17) | copy-start | bytes 9220
  826.9 52.3 %copy-start.33 = (f32[640]{0:T(1024)S(1)}, f32[640]{0:T(1024)}, u32[]{:S(2)}) copy-start(f32[640]{0:T(1024)} %copy-done.32) | copy-start | bytes 7684
  826.9 52.3 %copy-start.31 = (f32[640]{0:T(1024)S(1)}, f32[640]{0:T(1024)}, u32[]{:S(2)}) copy-start(f32[640]{0:T(1024)} %copy-done.30) | copy-start | bytes 7684
  827.0 54.6 %copy-start.13 = (bf16[640,768]{1,0:T(8,128)(2,1)S(1)}, bf16[640,768]{1,0:T(8,128)(2,1)}, u32[]{:S(2)}) copy-start(bf16[640,768]{1,0:T(8,128)(2,1)} %param.29) | copy-start | bytes 2949124
  (32 other events, 121.6 us)
Sparse Core Ops, SparseCore 0:
  14.4 79.1 all-gather.4
  135.4 134.8 reduce-scatter.4
  274.2 76.9 all-gather.6
  352.6 74.9 all-gather.8
  458.8 134.8 reduce-scatter.8
  595.8 73.1 reduce-scatter.6
  675.4 76.7 all-gather.10
  805.8 71.2 reduce-scatter.10
  881.9 114.5 all-reduce.4
where the time goes:
time: 1010 us
  waiting for transfers between devices  732 us (72%)
  matrix products  105 us (10%)
  local copies, waits for them, and re-layouts  62.3 us (6%)
  blocking collectives  56.1 us (6%)
  other arithmetic  38.2 us (4%)
  between operations  14.8 us (1%)
    reduce_scatter x1, waiting for transfers between devices, local(): lax.psum_scatter(jnp.dot(blend_low, mixer_weight, preferred_element_type=...  135 us
    reduce_scatter x1, waiting for transfers between devices, local(): lax.psum_scatter(jnp.einsum('rf,df->rd', grad_pre_low, up_weight, preferr...  120 us
    all_gather x1, waiting for transfers between devices, local(): whole_one = lax.all_gather(low_one, 'tensor', axis=0, tiled=True)  79 us
    all_gather x1, waiting for transfers between devices, local(): lax.all_gather(grad_first.astype(jnp.bfloat16), 'tensor', axis=0, tiled=T...  76.9 us
    all_gather x1, waiting for transfers between devices, local(): whole_two = lax.all_gather(low_two, 'tensor', axis=0, tiled=True)  76.5 us
    reduce_scatter x1, waiting for transfers between devices, local(): lax.psum_scatter(jnp.dot(active, down_weight, preferred_element_type=jnp....  73.1 us
    psum x1, waiting for transfers between devices, local(): lax.psum((weight_terms[0], weight_terms[1], weight_terms[2], weight_terms...  71.1 us
    all_gather x1, waiting for transfers between devices, local(): whole_grad = lax.all_gather(output_grad, 'tensor', axis=0, tiled=True)  67.5 us
  transfers between devices with their start and end apart: 9, of which 9 were waited for; matrix products, arithmetic and copies ran while one was open for 5% of the time, Pallas kernels for 0%

commit v1 on v0

--- a/solution.py
+++ b/solution.py
@@ -162,7 +162,17 @@
     inputs = tokens.astype(jnp.float32)
     grad_output = output_grad.astype(jnp.float32)
     low_one = layer_norm(inputs, norm_one_gain, norm_one_shift).astype(jnp.bfloat16)
-    whole_one = lax.all_gather(low_one, "tensor", axis=0, tiled=True)
+    size, index, extent = (lax.axis_size("tensor"), lax.axis_index("tensor"), low_one.shape[0])
+    right = [(i, (i + 1) % size) for i in range(size)]
+    whole_one = jnp.zeros(
+        (*low_one.shape[:0], size * extent, *low_one.shape[0 + 1 :]), low_one.dtype
+    )
+    block = low_one
+    for step in range(size):
+        source = (index - step) % size
+        whole_one = lax.dynamic_update_slice_in_dim(whole_one, block, source * extent, axis=0)
+        if step < size - 1:
+            block = lax.ppermute(block, "tensor", right)
     queries, key_rows, values = project_inputs(
         whole_one, input_weight, input_bias, slot_count, head_dim
     )

time: 1010 us -> 1010 us (level)
    all_gather x1 -> x0, waiting for transfers between devices: 79 us -> none  [local(): whole_one = lax.all_gather(low_one, 'tensor', axis=0, tiled=True)]
    ppermute x0 -> x3, waiting for transfers between devices: none -> 70.1 us  [local(): block = lax.ppermute(block, 'tensor', right)]
    unnamed x100 -> x108, local copies, waits for them, and re-layouts: 20.5 us -> 22.3 us
  transfers between devices with their start and end apart: 9 -> 11, of which waited for: 9 -> 11; matrix products, arithmetic and copies ran while one was open for 5% -> 6% of each run, Pallas kernels for 0% -> 0%
where the time goes in v1:
time: 1010 us
  waiting for transfers between devices  722 us (71%)
  matrix products  105 us (10%)
  local copies, waits for them, and re-layouts  68.7 us (7%)
  blocking collectives  56.1 us (6%)
  other arithmetic  36.1 us (4%)
  between operations  15.1 us (1%)
    reduce_scatter x1, waiting for transfers between devices, local(): lax.psum_scatter(jnp.dot(blend_low, mixer_weight, preferred_element_type=...  134 us
    reduce_scatter x1, waiting for transfers between devices, local(): lax.psum_scatter(jnp.einsum('rf,df->rd', grad_pre_low, up_weight, preferr...  120 us
    all_gather x1, waiting for transfers between devices, local(): lax.all_gather(grad_first.astype(jnp.bfloat16), 'tensor', axis=0, tiled=T...  76.9 us
    all_gather x1, waiting for transfers between devices, local(): whole_two = lax.all_gather(low_two, 'tensor', axis=0, tiled=True)  76.3 us
    reduce_scatter x1, waiting for transfers between devices, local(): lax.psum_scatter(jnp.dot(active, down_weight, preferred_element_type=jnp....  73 us
    psum x1, waiting for transfers between devices, local(): lax.psum((weight_terms[0], weight_terms[1], weight_terms[2], weight_terms...  71.1 us
    ppermute x3, waiting for transfers between devices, local(): block = lax.ppermute(block, 'tensor', right)  70.1 us
    all_gather x1, waiting for transfers between devices, local(): whole_grad = lax.all_gather(output_grad, 'tensor', axis=0, tiled=True)  67.6 us
  transfers between devices with their start and end apart: 11, of which 11 were waited for; matrix products, arithmetic and copies ran while one was open for 6% of the time, Pallas kernels for 0%

profile of v1, /device:TPU:0, one launch (start us, length us, event | category | flops | bytes accessed | tf_op | source)
XLA Modules:
  0.0 1007.5 jit_solution(4701065699389302121)
XLA Ops:
  16.7 23.8 %collective-permute-done = bf16[640,768]{1,0:T(8,128)(2,1)S(1)} collective-permute-done((bf16[640,768]{1,0:T(8,128)(2,1)S(1)}, bf16[640,768]{1,0:T(8,128)(2,1)S(1)}, u32[]{:S(2)}, u32[]{:S(2)}) %collective-permute-start) | collective-permute-done | bytes 983072 | tf_op jit(solution)/shard_map/ppermute | solution.py:175
  40.5 24.7 %collective-permute-done.1 = bf16[640,768]{1,0:T(8,128)(2,1)S(1)} collective-permute-done((bf16[640,768]{1,0:T(8,128)(2,1)S(1)}, bf16[640,768]{1,0:T(8,128)(2,1)S(1)}, u32[]{:S(2)}, u32[]{:S(2)}) %collective-permute-start.1) | collective-permute-done | bytes 983072 | tf_op jit(solution)/shard_map/ppermute | solution.py:175
  67.6 21.6 %collective-permute-done.2 = bf16[640,768]{1,0:T(8,128)(2,1)} collective-permute-done((bf16[640,768]{1,0:T(8,128)(2,1)S(1)}, bf16[640,768]{1,0:T(8,128)(2,1)}, u32[]{:S(2)}, u32[]{:S(2)}) %collective-permute-start.2) | collective-permute-done | bytes 983072 | tf_op jit(solution)/shard_map/ppermute | solution.py:175
  102.5 4.7 squeeze.4
  111.4 5.2 fusion.58
  133.1 134.1 %reduce-scatter.5.cloned.1.call-done = f32[640,768]{1,0:T(8,128)} async-done(((f32[2560,768]{1,0:T(8,128)}), f32[640,768]{1,0:T(8,128)}) %reduce-scatter.5.cloned.1.call-update) | async-done | bytes 1966096 | tf_op jit(solution)/shard_map/reduce_scatter | solution.py:183
  271.9 76.3 %all-gather.4.cloned.1.call-done = bf16[2560,768]{1,0:T(8,128)(2,1)} async-done(((bf16[640,768]{1,0:T(8,128)(2,1)}), bf16[2560,768]{1,0:T(8,128)(2,1)}) %all-gather.4.cloned.1.call-update) | async-done | bytes 3932176 | tf_op jit(solution)/shard_map/all_gather | solution.py:192
  348.1 9.0 fusion.60
  357.1 67.6 %all-gather.6.cloned.1.call-done = bf16[2560,768]{1,0:T(8,128)(2,1)} async-done(((bf16[640,768]{1,0:T(8,128)(2,1)}), bf16[2560,768]{1,0:T(8,128)(2,1)}) %all-gather.6.cloned.1.call-update) | async-done | bytes 3932176 | tf_op jit(solution)/shard_map/all_gather | solution.py:205
  424.8 23.8 %fusion.51 = (f32[768]{0:T(1024)S(1)}, bf16[2560,768]{1,0:T(8,128)(2,1)S(1)}, f32[2560,768]{1,0:T(8,128)}) fusion(f32[2560,768]{1,0:T(8,128)} %fusion.60, f32[768]{0:T(1024)S(1)} %convert_element_type.88, bf16[2560,768]{1,0:T(8,128)(2,1)} %all-gather.6.cloned.1.call-done, bf16[768,768]{1,0:T(8,128)(2,1)S(1)} %copy-done), kind=kOutput, calls=%fused_computation.110 | convolution fusion | flops 3165388032 | bytes 24778752 | tf_op jit(solution)/shard_map/rd,fd->rf/dot_general | solution.py:100
  450.4 5.3 fusion.29
  456.3 8.0 multiply_convert_fusion
  466.2 4.7 convolution_convert_fusion
  471.0 119.8 %reduce-scatter.9.cloned.1.call-done = f32[640,768]{1,0:T(8,128)} async-done(((f32[2560,768]{1,0:T(8,128)}), f32[640,768]{1,0:T(8,128)}) %reduce-scatter.9.cloned.1.call-update) | async-done | bytes 1966096 | tf_op jit(solution)/shard_map/reduce_scatter | solution.py:209
  593.1 73.0 %reduce-scatter.7.cloned.1.call-done = bf16[640,768]{1,0:T(8,128)(2,1)} async-done(((bf16[2560,768]{1,0:T(8,128)(2,1)}), bf16[640,768]{1,0:T(8,128)(2,1)}) %reduce-scatter.7.cloned.1.call-update) | async-done | bytes 983056 | tf_op jit(solution)/shard_map/reduce_scatter | solution.py:197
  672.4 76.9 %all-gather.8.cloned.1.call-done = bf16[2560,768]{1,0:T(8,128)(2,1)} async-done(((bf16[640,768]{1,0:T(8,128)(2,1)}), bf16[2560,768]{1,0:T(8,128)(2,1)}) %all-gather.8.cloned.1.call-update) | async-done | bytes 3932176 | tf_op jit(solution)/shard_map/all_gather | solution.py:219
  757.0 7.1 multiply_reduce_fusion
  798.0 4.8 bitcast_convert_fusion
  803.1 8.1 fusion.27
  811.3 4.8 fusion.62
  827.1 14.4 %all-reduce.1 = (f32[2,192]{1,0:T(2,128)}, f32[768]{0:T(1024)}) all-reduce(f32[2,192]{1,0:T(2,128)S(1)} %pad_maximum_fusion, f32[768]{0:T(1024)S(1)} %get-tuple-element.37), channel_id=1, replica_groups=mesh['dp'=8,'tensor'=4] {'dp'}, use_global_device_ids=true, to_apply=%region_22.23 | all-reduce | flops 1152 | bytes 9216 | tf_op jit(solution)/shard_map/psum | solution.py:259
  841.5 32.7 %reduce-scatter.11.cloned.1.call-done = bf16[640,768]{1,0:T(8,128)(2,1)} async-done(((bf16[2560,768]{1,0:T(8,128)(2,1)}), bf16[640,768]{1,0:T(8,128)(2,1)}) %reduce-scatter.11.cloned.1.call-update) | async-done | bytes 983056 | tf_op jit(solution)/shard_map/reduce_scatter | solution.py:233
  880.9 41.7 %all-reduce = (f32[768]{0:T(1024)}, f32[768]{0:T(1024)}, f32[768]{0:T(1024)}, f32[768]{0:T(1024)}, f32[768]{0:T(1024)}, /*index=5*/f32[768]{0:T(1024)}) all-reduce(f32[768]{0:T(1024)S(1)} %get-tuple-element.16, f32[768]{0:T(1024)S(1)} %get-tuple-element.21, ...), channel_id=1, replica_groups=mesh['dp'=8,'tensor'=4] {'dp','tensor'}, use_global_device_ids=true, to_apply=%region_16.17 | all-reduce | flops 4608 | bytes 36864 | tf_op jit(solution)/shard_map/psum | solution.py:247
  922.5 71.1 %all-reduce.5.cloned.1.call-done = (f32[768,3,192]{0,2,1:T(8,128)}, f32[192,768]{1,0:T(8,128)}, f32[768,768]{1,0:T(8,128)}, f32[768,768]{1,0:T(8,128)}) async-done(((f32[768,3,192]{0,2,1:T(8,128)}, f32[192,768]{1,0:T(8,128)}, f32[768,768]{1,0:T(8,128)}, f32[768,768]{1,0:T(8,128)}), (f32[768,3,192]{0,2,1:T(8,128)}, f32[192,768]{1,0:T(8,128)}, f32[768,768]{1,0:T(8,128)}, ...) | async-done | bytes 7077904 | tf_op jit(solution)/shard_map/psum | solution.py:259
  (187 shorter events, 129.2 us)
Async XLA Ops:
  7.2 417.6 %copy-start = (bf16[768,768]{1,0:T(8,128)(2,1)S(1)}, bf16[768,768]{1,0:T(8,128)(2,1)}, u32[]{:S(2)}) copy-start(bf16[768,768]{1,0:T(8,128)(2,1)} %param.27) | copy-start | bytes 3538948
  7.2 260.0 %reduce-scatter.5.cloned.1.call-start = ((), (), s32[]{:S(2)}) async-start(), calls=%async_computation.4 | async-start | bytes 9830400 | tf_op jit(solution)/shard_map/reduce_scatter | solution.py:183
  11.1 54.2 %copy-start.43 = (bf16[2,192]{1,0:T(2,128)(2,1)S(1)}, bf16[2,192]{1,0:T(2,128)(2,1)}, u32[]{:S(2)}) copy-start(bf16[2,192]{1,0:T(2,128)(2,1)} %param.20) | copy-start | bytes 2308
  11.1 54.4 %copy-start.45 = (s32[32]{0:T(128)S(1)}, s32[32]{0:T(128)}, u32[]{:S(2)}) copy-start(s32[32]{0:T(128)} %param.16) | copy-start | bytes 388
  13.7 26.8 %collective-permute-start = (bf16[640,768]{1,0:T(8,128)(2,1)S(1)}, bf16[640,768]{1,0:T(8,128)(2,1)S(1)}, u32[]{:S(2)}, u32[]{:S(2)}) collective-permute-start(bf16[640,768]{1,0:T(8,128)(2,1)S(1)} %get-tuple-element.45), channel_id=1, source_target_pairs={{0,1},{1,2},{2,3},{3,0},{4,5},{5,6},{6,7},{7,4},{8,9},{9,10},{10,1... | collective-permute-start | bytes 2949128 | tf_op jit(solution)/shard_map/ppermute | solution.py:175
  40.5 24.7 %collective-permute-start.1 = (bf16[640,768]{1,0:T(8,128)(2,1)S(1)}, bf16[640,768]{1,0:T(8,128)(2,1)S(1)}, u32[]{:S(2)}, u32[]{:S(2)}) collective-permute-start(bf16[640,768]{1,0:T(8,128)(2,1)S(1)} %collective-permute-done), channel_id=1, source_target_pairs={{0,1},{1,2},{2,3},{3,0},{4,5},{5,6},{6,7},{7,4},{8,9},{9,10},{10,1... | collective-permute-start | bytes 2949128 | tf_op jit(solution)/shard_map/ppermute | solution.py:175
  65.3 23.9 %collective-permute-start.2 = (bf16[640,768]{1,0:T(8,128)(2,1)S(1)}, bf16[640,768]{1,0:T(8,128)(2,1)}, u32[]{:S(2)}, u32[]{:S(2)}) collective-permute-start(bf16[640,768]{1,0:T(8,128)(2,1)S(1)} %collective-permute-done.1), channel_id=1, source_target_pairs={{0,1},{1,2},{2,3},{3,0},{4,5},{5,6},{6,7},{7,4},{8,9},{9,10},{10,1... | collective-permute-start | bytes 2949128 | tf_op jit(solution)/shard_map/ppermute | solution.py:175
  133.0 134.2 %copy-start.40 = (f32[768]{0:T(1024)S(1)}, f32[768]{0:T(1024)}, u32[]{:S(2)}) copy-start(f32[768]{0:T(1024)} %param.22) | copy-start | bytes 9220
  133.1 136.6 %copy-start.38 = (f32[768]{0:T(1024)S(1)}, f32[768]{0:T(1024)}, u32[]{:S(2)}) copy-start(f32[768]{0:T(1024)} %param.23) | copy-start | bytes 9220
  133.1 136.6 %copy-start.41 = (f32[768]{0:T(1024)S(1)}, f32[768]{0:T(1024)}, u32[]{:S(2)}) copy-start(f32[768]{0:T(1024)} %param.24) | copy-start | bytes 9220
  133.1 215.1 %all-gather.4.cloned.1.call-start = ((), (), s32[]{:S(2)}) async-start(), calls=%async_computation.5 | async-start | bytes 4915200 | tf_op jit(solution)/shard_map/all_gather | solution.py:192
  271.0 153.7 %all-gather.6.cloned.1.call-start = ((), (), s32[]{:S(2)}) async-start(), calls=%async_computation.7 | async-start | bytes 4915200 | tf_op jit(solution)/shard_map/all_gather | solution.py:205
  271.8 319.0 %reduce-scatter.9.cloned.1.call-start = ((), (), s32[]{:S(2)}) async-start(), calls=%async_computation.8 | async-start | bytes 9830400 | tf_op jit(solution)/shard_map/reduce_scatter | solution.py:209
  455.8 210.3 %reduce-scatter.7.cloned.1.call-start = ((), (), s32[]{:S(2)}) async-start(), calls=%async_computation.6 | async-start | bytes 4915200 | tf_op jit(solution)/shard_map/reduce_scatter | solution.py:197
  470.9 195.2 %copy-start.42 = (f32[768]{0:T(1024)S(1)}, f32[768]{0:T(1024)}, u32[]{:S(2)}) copy-start(f32[768]{0:T(1024)} %param.28) | copy-start | bytes 9220
  470.9 278.3 %all-gather.8.cloned.1.call-start = ((), (), s32[]{:S(2)}) async-start(), calls=%async_computation.9 | async-start | bytes 4915200 | tf_op jit(solution)/shard_map/all_gather | solution.py:219
  672.3 201.9 %reduce-scatter.11.cloned.1.call-start = ((), (), s32[]{:S(2)}) async-start(), calls=%async_computation.10 | async-start | bytes 4915200 | tf_op jit(solution)/shard_map/reduce_scatter | solution.py:233
  802.8 190.8 %all-reduce.5.cloned.1.call-start = ((), (), s32[]{:S(2)}) async-start(), calls=%async_computation.11 | async-start | bytes 14155776 | tf_op jit(solution)/shard_map/psum | solution.py:259
  822.2 52.0 %copy-start.4 = (bf16[640,768]{1,0:T(8,128)(2,1)S(1)}, bf16[640,768]{1,0:T(8,128)(2,1)}, u32[]{:S(2)}) copy-start(bf16[640,768]{1,0:T(8,128)(2,1)} %param.15) | copy-start | bytes 2949124
  822.2 52.0 %copy-start.31 = (f32[640]{0:T(1024)S(1)}, f32[640]{0:T(1024)}, u32[]{:S(2)}) copy-start(f32[640]{0:T(1024)} %copy-done.30) | copy-start | bytes 7684
  822.2 52.0 %copy-start.33 = (f32[768]{0:T(1024)S(1)}, f32[768]{0:T(1024)}, u32[]{:S(2)}) copy-start(f32[768]{0:T(1024)} %param.17) | copy-start | bytes 9220
  824.5 51.8 %copy-start.37 = (f32[640]{0:T(1024)S(1)}, f32[640]{0:T(1024)}, u32[]{:S(2)}) copy-start(f32[640]{0:T(1024)} %copy-done.36) | copy-start | bytes 7684
  824.5 51.8 %copy-start.35 = (f32[640]{0:T(1024)S(1)}, f32[640]{0:T(1024)}, u32[]{:S(2)}) copy-start(f32[640]{0:T(1024)} %copy-done.34) | copy-start | bytes 7684
  824.6 54.1 %copy-start.14 = (bf16[640,768]{1,0:T(8,128)(2,1)S(1)}, bf16[640,768]{1,0:T(8,128)(2,1)}, u32[]{:S(2)}) copy-start(bf16[640,768]{1,0:T(8,128)(2,1)} %param.29) | copy-start | bytes 2949124
  (38 other events, 191.6 us)
Sparse Core Ops, SparseCore 0:
  133.2 133.9 reduce-scatter.4
  271.2 76.9 all-gather.3
  349.7 74.9 all-gather.5
  455.9 134.8 reduce-scatter.8
  592.9 73.1 reduce-scatter.6
  672.5 76.7 all-gather.7
  802.9 71.2 reduce-scatter.10
  879.0 114.5 all-reduce.4
